TPU v7x, 32 devices: a whole 2x2x4 slice. The times are simulated.
32 devices in a mesh: row: 4 (over y, x), col: 8 (over z, core).
Axes of the slice: x: 2, y: 2, z: 4, core: 2. Of those that a mesh axis runs over, the one named last changes fastest.
Arguments:
- inputs: bfloat16 [2048, 25600], P('row', 'col'), may hold values from -6 to 6
- out_grads: bfloat16 [2048, 5120], P('col', 'row'), may hold values from -0.125 to 0.125
- weights: bfloat16 [5120, 25600], P('row', 'col'), may hold values from -3 to 3
- momentum: float32 [5120, 25600], P('row', 'col'), may hold values from -13 to 13
- right_factor: float32 [25600, 256], P('col'), may hold values from -6 to 6
Outputs:
- weights_new: float32 [5120, 25600], P('row', 'col')
- momentum_new: float32 [5120, 25600], P('row', 'col')
- factor_new: float32 [25600, 256], P('col')
All inputs are finite; a program needn't handle non-finite values.
Results may differ from a plain program's by a relative error of at most 0.0003.
Values may be sent and summed in bfloat16 or wider, within the bound.
No kernel may reach another device: no remote copies, remote signals or barrier semaphores. Data moves between devices by JAX's collectives and lax.ppermute only.
A program may use at most 128 MiB of HBM per device.

v0:
```python
import math
import jax
import jax.numpy as jnp
from jax import lax
from jax.sharding import PartitionSpec as P

M = 5120
N = 25600
RANK = 256
mix_rate = 0.95
step_rate = 0.3
weight_decay = 0.1
tiny_eps = 1e-06
highest = lax.Precision.HIGHEST


def inner_rows(left_side, right_in):
    return lax.dot_general(left_side, right_in, (((0,), (0,)), ((), ())), precision=highest)


def orthonormal(sketch_rows, gram_total):
    factor_low = jnp.linalg.cholesky(gram_total)
    return jax.scipy.linalg.solve_triangular(factor_low, sketch_rows.T, lower=True).T


def on_device(inputs, out_grads, weights, momentum, right_factor):
    grads_all = lax.all_gather(out_grads, "col", axis=0, tiled=True)
    gradient = lax.dot_general(
        grads_all,
        lax.all_gather(inputs, "row", axis=0, tiled=True),
        (((0,), (0,)), ((), ())),
        preferred_element_type=jnp.float32,
    )
    moment = momentum + gradient
    sketch_part = jnp.dot(moment, right_factor, precision=highest)
    sketch_rows = lax.psum(sketch_part, "col")
    gram_total = lax.psum(inner_rows(sketch_rows, sketch_rows), "row")
    basis_rows = orthonormal(sketch_rows, gram_total)
    right_part = inner_rows(moment, basis_rows)
    right_share = lax.psum_scatter(right_part, "row", scatter_dimension=0, tiled=True)
    squares = lax.psum(jnp.sum(right_share * right_share, axis=0), ("row", "col"))
    right_side = lax.all_gather(right_share, "row", axis=0, tiled=True)
    column_scale = lax.rsqrt(squares / N + tiny_eps)
    factor_new = right_side * column_scale
    momentum_new = moment - (1.0 - mix_rate) * jnp.dot(basis_rows, right_side.T, precision=highest)
    update = jnp.dot(basis_rows, factor_new.T, precision=highest)
    weights_new = (
        weights.astype(jnp.float32) * (1.0 - step_rate * weight_decay)
        - step_rate * math.sqrt(M / RANK) * update
    )
    return (weights_new, momentum_new, factor_new)


def solution(mesh):
    placed = (P("row", "col"), P("col", "row"), P("row", "col"), P("row", "col"), P("col", None))
    return jax.shard_map(
        on_device,
        mesh=mesh,
        in_specs=placed,
        out_specs=(P("row", "col"), P("row", "col"), P("col", None)),
        check_vma=False,
    )
```

profile of v0, /device:TPU:0, one launch (start us, length us, event | category | flops | bytes accessed | tf_op | source)
XLA Modules:
  0.0 616.2 jit_solution(3706774686516627048)
XLA Ops:
  7.2 0.0 copy-start
  7.2 0.0 all-gather.4.cloned.1.call-start
  7.2 0.7 all-gather.4.cloned.1.call-update
  7.9 0.0 all-gather.6.cloned.1.call-start
  8.0 0.7 all-gather.6.cloned.1.call-update
  8.7 0.0 all-reduce.4.cloned.1.call-start
  8.7 59.7 %all-gather.4.cloned.1.call-done = bf16[2048,1280]{1,0:T(8,128)(2,1)} async-done(((bf16[256,1280]{1,0:T(8,128)(2,1)}), bf16[2048,1280]{1,0:T(8,128)(2,1)}) %all-gather.4.cloned.1.call-update) | async-done | bytes 5242896 | tf_op jit(solution)/shard_map/all_gather | solution.py:27
  68.4 127.4 %all-gather.6.cloned.1.call-done = bf16[2048,3200]{1,0:T(8,128)(2,1)} async-done(((bf16[512,3200]{1,0:T(8,128)(2,1)}), bf16[2048,3200]{1,0:T(8,128)(2,1)}) %all-gather.6.cloned.1.call-update) | async-done | bytes 13107216 | tf_op jit(solution)/shard_map/all_gather | solution.py:30
  195.8 29.4 %convolution_add_fusion = f32[1280,3200]{1,0:T(8,128)} fusion(f32[1280,3200]{1,0:T(8,128)} %param.8, bf16[2048,1280]{1,0:T(8,128)(2,1)} %all-gather.4.cloned.1.call-done, bf16[2048,3200]{1,0:T(8,128)(2,1)} %all-gather.6.cloned.1.call-done), kind=kOutput, calls=%fused_computation.2 | convolution fusion | flops 16781312000 | bytes 51118080 | tf_op jit(solution)/shard_map/dot_general | solution.py:28
  225.1 0.0 copy-done
  225.1 17.8 %fusion.15 = f32[1280,256]{1,0:T(8,128)} fusion(f32[1280,3200]{1,0:T(8,128)} %convolution_add_fusion, f32[3200,256]{1,0:T(8,128)S(1)} %copy-done), kind=kOutput, calls=%fused_computation.41 | convolution fusion | flops 12582912000 | bytes 20971520 | tf_op jit(solution)/shard_map/dot_general | solution.py:35
  242.9 0.0 all-reduce.4.cloned.1.call-update
  242.9 0.0 all-reduce.6.cloned.1.call-start
  243.0 60.5 %all-reduce.4.cloned.1.call-done = f32[1280,256]{1,0:T(8,128)} async-done(((f32[1280,256]{1,0:T(8,128)}), f32[1280,256]{1,0:T(8,128)}) %all-reduce.4.cloned.1.call-update) | async-done | bytes 1310736 | tf_op jit(solution)/shard_map/psum | solution.py:36
  303.5 0.0 copy-start.5
  303.5 4.8 fusion.16
  308.3 0.0 all-reduce.6.cloned.1.call-update
  308.4 0.2 reduce-scatter.2.cloned.1.call-start
  308.6 42.0 %all-reduce.6.cloned.1.call-done = f32[256,256]{0,1:T(8,128)} async-done(((f32[256,256]{0,1:T(8,128)}), f32[256,256]{0,1:T(8,128)}) %all-reduce.6.cloned.1.call-update) | async-done | bytes 262160 | tf_op jit(solution)/shard_map/psum | solution.py:37
  350.6 1.1 copy.9
  351.7 1.0 fusion.5
  352.7 11.7 %cholesky.50 = f32[128,128]{1,0:T(8,128)S(1)} custom-call(f32[128,128]{1,0:T(8,128)S(1)} %cholesky.118), custom_call_target="Cholesky" | custom-call | tf_op jit(solution)/shard_map/jit(cholesky)/cholesky | solution.py:22
  364.4 9.8 %custom-call.15 = f32[1,128,128]{1,2,0:T(8,128)S(1)} custom-call(f32[1,128,128]{2,1,0:T(8,128)S(1)} %get-tuple-element.24), custom_call_target="InvertDiagBlocksLowerTriangular" | custom-call | tf_op jit(solution)/shard_map/jit(cholesky)/cholesky | solution.py:22
  374.3 0.2 constant_dynamic-update-slice_fusion.1
  374.5 0.3 convolution_subtract_fusion.1
  374.8 11.7 %cholesky.105 = f32[128,128]{1,0:T(8,128)S(1)} custom-call(f32[128,128]{1,0:T(8,128)S(1)} %convolution_subtract_fusion.1), custom_call_target="Cholesky" | custom-call | tf_op jit(solution)/shard_map/jit(cholesky)/cholesky | solution.py:22
  386.5 0.7 compare_reduce_fusion
  388.6 0.1 triangular_solve.57
  388.6 4.2 while.1
  388.8 0.6 fusion.31
  389.4 1.4 bitcast_dynamic-update-slice_fusion.2
  390.8 0.6 fusion.31
  391.4 1.4 bitcast_dynamic-update-slice_fusion.2
  392.8 19.7 %custom-call.16 = f32[2,128,128]{1,2,0:T(8,128)S(1)} custom-call(f32[2,128,128]{2,1,0:T(8,128)S(1)} %get-tuple-element.10), custom_call_target="InvertDiagBlocksLowerTriangular" | custom-call | tf_op jit(solution)/shard_map/jit(_solve_triangular)/triangular_solve | solution.py:23
  412.5 0.0 copy-done.5
  412.5 0.8 fusion.3
  413.3 0.0 copy-start.2
  413.3 1.2 convolution_subtract_fusion
  414.5 0.8 fusion.7
  415.2 0.0 copy-start.6
  415.2 32.1 %fusion.2 = f32[3200,256]{1,0:T(8,128)} fusion(f32[1280,3200]{1,0:T(8,128)} %convolution_add_fusion, f32[128,1280]{1,0:T(8,128)S(1)} %fusion.7, f32[128,1280]{1,0:T(8,128)S(1)} %fusion.3), kind=kOutput, calls=%fused_computation.11 | convolution fusion | flops 12583239680 | bytes 20971520 | tf_op jit(solution)/shard_map/dot_general | solution.py:18
  447.4 0.0 reduce-scatter.2.cloned.1.call-update
  447.4 0.0 all-gather.8.cloned.1.call-start
  447.4 45.1 %reduce-scatter.2.cloned.1.call-done = f32[800,256]{1,0:T(8,128)} async-done(((f32[3200,256]{1,0:T(8,128)}), f32[800,256]{1,0:T(8,128)}) %reduce-scatter.2.cloned.1.call-update) | async-done | bytes 819216 | tf_op jit(solution)/shard_map/reduce_scatter | solution.py:40
  492.5 0.0 all-gather.8.cloned.1.call-update
  492.6 1.3 multiply_reduce_fusion
  493.8 40.3 %psum.23 = f32[256]{0:T(256)S(1)} all-reduce(f32[256]{0:T(256)S(1)} %multiply_reduce_fusion), channel_id=1, replica_groups=mesh['row'=4,'col'=8] {'row','col'}, use_global_device_ids=true, to_apply=%region_8.9 | all-reduce | flops 256 | bytes 2048 | tf_op jit(solution)/shard_map/psum | solution.py:41
  534.1 6.0 all-gather.8.cloned.1.call-done
  540.1 2.1 broadcast_multiply_fusion
  542.2 0.0 copy-done.2
  542.2 0.0 copy-done.6
  542.2 0.0 copy-start.3
  542.3 0.0 copy-start.4
  542.3 32.8 %fusion.1 = f32[1280,3200]{1,0:T(8,128)} fusion(f32[3200,256]{1,0:T(8,128)S(1)} %broadcast_multiply_fusion, bf16[1280,3200]{1,0:T(8,128)(2,1)} %param.7, f32[128,1280]{1,0:T(8,128)S(1)} %fusion.7, f32[128,1280]{1,0:T(8,128)S(1)} %fusion.3), kind=kOutput, calls=%fused_computation.6 | convolution fusion | flops 12599623680 | bytes 29163520 | tf_op jit(solution)/shard_map/dot_general | solution.py:46
  575.0 0.0 copy-done.3
  575.0 0.0 copy-done.4
  575.0 0.0 copy-start.1
  575.0 34.1 %fusion = f32[1280,3200]{1,0:T(8,128)} fusion(f32[1280,3200]{1,0:T(8,128)} %convolution_add_fusion, f32[3200,256]{1,0:T(8,128)S(1)} %copy-done.4, f32[128,1280]{1,0:T(8,128)} %copy-done.6, f32[128,1280]{1,0:T(8,128)} %copy-done.2), kind=kOutput, calls=%fused_computation.4 | convolution fusion | flops 12591431680 | bytes 37355520 | tf_op jit(solution)/shard_map/dot_general | solution.py:45
  609.1 0.0 copy-done.1
  (10 shorter events, 0.2 us)
Async XLA Ops:
  7.2 217.9 %copy-start = (f32[3200,256]{1,0:T(8,128)S(1)}, f32[3200,256]{1,0:T(8,128)}, u32[]{:S(2)}) copy-start(f32[3200,256]{1,0:T(8,128)} %param.9) | copy-start | bytes 9830404
  7.2 61.2 %all-gather.4.cloned.1.call-start = ((), (), s32[]{:S(2)}) async-start(), calls=%async_computation.1 | async-start | bytes 5898240 | tf_op jit(solution)/shard_map/all_gather | solution.py:27
  7.9 187.8 %all-gather.6.cloned.1.call-start = ((), (), s32[]{:S(2)}) async-start(), calls=%async_computation.2 | async-start | bytes 16384000 | tf_op jit(solution)/shard_map/all_gather | solution.py:30
  8.7 294.8 %all-reduce.4.cloned.1.call-start = ((), (), s32[]{:S(2)}) async-start(), calls=%async_computation.3 | async-start | bytes 2621440 | tf_op jit(solution)/shard_map/psum | solution.py:36
  242.9 107.7 %all-reduce.6.cloned.1.call-start = ((), (), s32[]{:S(2)}) async-start(), calls=%async_computation.4 | async-start | bytes 524288 | tf_op jit(solution)/shard_map/psum | solution.py:37
  303.5 109.0 %copy-start.5 = (f32[1280,256]{1,0:T(8,128)S(1)}, f32[1280,256]{1,0:T(8,128)}, u32[]{:S(2)}) copy-start(f32[1280,256]{1,0:T(8,128)} %all-reduce.4.cloned.1.call-done) | copy-start | bytes 3932164
  308.4 184.2 %reduce-scatter.2.cloned.1.call-start = ((), (), s32[]{:S(2)}) async-start(), calls=%async_computation.5 | async-start | bytes 4096000 | tf_op jit(solution)/shard_map/reduce_scatter | solution.py:40
  413.3 129.0 %copy-start.2 = (f32[128,1280]{1,0:T(8,128)}, f32[128,1280]{1,0:T(8,128)S(1)}, u32[]{:S(2)}) copy-start(f32[128,1280]{1,0:T(8,128)S(1)} %fusion.3) | copy-start | bytes 1966084
  415.2 127.0 %copy-start.6 = (f32[128,1280]{1,0:T(8,128)}, f32[128,1280]{1,0:T(8,128)S(1)}, u32[]{:S(2)}) copy-start(f32[128,1280]{1,0:T(8,128)S(1)} %fusion.7) | copy-start | bytes 1966084
  447.4 92.7 %all-gather.8.cloned.1.call-start = ((), (), s32[]{:S(2)}) async-start(), calls=%async_computation.6 | async-start | bytes 4096000 | tf_op jit(solution)/shard_map/all_gather | solution.py:42
  542.2 32.8 %copy-start.3 = (f32[3200,256]{1,0:T(8,128)}, f32[3200,256]{1,0:T(8,128)S(1)}, u32[]{:S(2)}) copy-start(f32[3200,256]{1,0:T(8,128)S(1)} %broadcast_multiply_fusion) | copy-start | bytes 9830404
  542.3 32.8 %copy-start.4 = (f32[3200,256]{1,0:T(8,128)S(1)}, f32[3200,256]{1,0:T(8,128)}, u32[]{:S(2)}) copy-start(f32[3200,256]{1,0:T(8,128)} %all-gather.8.cloned.1.call-done) | copy-start | bytes 9830404
  575.0 34.1 %copy-start.1 = (f32[3200,256]{1,0:T(8,128)S(1)}, f32[3200,256]{1,0:T(8,128)}, u32[]{:S(2)}) copy-start(f32[3200,256]{1,0:T(8,128)} %param.9) | copy-start | bytes 9830404
Sparse Core Ops, SparseCore 0:
  9.6 58.6 all-gather.3
  70.2 125.5 all-gather.5
  243.0 60.4 all-reduce.3
  308.5 42.0 all-reduce.5
  447.5 44.9 reduce-scatter.1
  494.2 45.7 all-gather.7
where the time goes:
time: 623 us; the launch traced here: 616 us
  waiting for transfers between devices  342 us (55%)
  matrix products  154 us (25%)
  other arithmetic  58.1 us (9%)
  blocking collectives  40.3 us (6%)
  between operations  15.8 us (3%)
    all_gather x1, waiting for transfers between devices, on_device(): lax.all_gather(inputs, 'row', axis=0, tiled=True)  127 us
    psum x1, waiting for transfers between devices, on_device(): sketch_rows = lax.psum(sketch_part, 'col')  60.5 us
    all_gather x1, waiting for transfers between devices, on_device(): grads_all = lax.all_gather(out_grads, 'col', axis=0, tiled=True)  59.7 us
    reduce_scatter x1, waiting for transfers between devices, on_device(): lax.psum_scatter(right_part, 'row', scatter_dimension=0, tiled=True)  45.1 us
    psum x1, waiting for transfers between devices, on_device(): gram_total = lax.psum(inner_rows(sketch_rows, sketch_rows), 'row')  42 us
    psum x1, blocking collectives, on_device(): lax.psum(jnp.sum(right_share * right_share, axis=0), ('row', 'col'))  40.3 us
    dot_general x2, matrix products, inner_rows(): lax.dot_general(left_side, right_in, (((0,), (0,)), ((), ())), precision=...  36.9 us
    dot_general x1, matrix products, on_device(): jnp.dot(basis_rows, right_side.T, precision=highest)  34.1 us
  transfers between devices with their start and end apart: 6, of which 6 were waited for; matrix products, arithmetic and copies ran while one was open for 0% of the time, Pallas kernels for 0%

commit v1 on v0

--- a/solution.py
+++ b/solution.py
@@ -1,3 +1,4 @@
+import functools
 import math
 import jax
 import jax.numpy as jnp
@@ -12,6 +13,13 @@
 weight_decay = 0.1
 tiny_eps = 1e-06
 highest = lax.Precision.HIGHEST
+
+
+def solve_entries(message, dev_axis, comm_axis):
+    return lax.psum(lax.psum(message, dev_axis), comm_axis)
+
+
+answer_squares = functools.partial(solve_entries, dev_axis="col", comm_axis="row")
 
 
 def inner_rows(left_side, right_in):
@@ -38,7 +46,7 @@
     basis_rows = orthonormal(sketch_rows, gram_total)
     right_part = inner_rows(moment, basis_rows)
     right_share = lax.psum_scatter(right_part, "row", scatter_dimension=0, tiled=True)
-    squares = lax.psum(jnp.sum(right_share * right_share, axis=0), ("row", "col"))
+    squares = answer_squares(jnp.sum(right_share * right_share, axis=0))
     right_side = lax.all_gather(right_share, "row", axis=0, tiled=True)
     column_scale = lax.rsqrt(squares / N + tiny_eps)
     factor_new = right_side * column_scale

time: 623 us -> 623 us (level)
  blocking collectives: 40.3 us -> 25.1 us
  waiting for transfers between devices: 342 us -> 356 us
    psum x1 -> x2, blocking collectives: 40.3 us -> 25.1 us  [solve_entries(): return lax.psum(lax.psum(message, dev_axis), comm_axis)]
    all_gather x1, waiting for transfers between devices: 5.98 us -> 20.3 us  [on_device(): right_side = lax.all_gather(right_share, 'row', axis=0, tiled=True)]
where the time goes in v1:
time: 623 us; the launch traced here: 616 us
  waiting for transfers between devices  356 us (57%)
  matrix products  154 us (25%)
  other arithmetic  58.1 us (9%)
  blocking collectives  25.1 us (4%)
  between operations  15.8 us (3%)
    all_gather x1, waiting for transfers between devices, on_device(): lax.all_gather(inputs, 'row', axis=0, tiled=True)  127 us
    psum x1, waiting for transfers between devices, on_device(): sketch_rows = lax.psum(sketch_part, 'col')  60.5 us
    all_gather x1, waiting for transfers between devices, on_device(): grads_all = lax.all_gather(out_grads, 'col', axis=0, tiled=True)  59.7 us
    reduce_scatter x1, waiting for transfers between devices, on_device(): lax.psum_scatter(right_part, 'row', scatter_dimension=0, tiled=True)  45.1 us
    psum x1, waiting for transfers between devices, on_device(): gram_total = lax.psum(inner_rows(sketch_rows, sketch_rows), 'row')  42 us
    dot_general x2, matrix products, inner_rows(): lax.dot_general(left_side, right_in, (((0,), (0,)), ((), ())), precision=...  36.9 us
    dot_general x1, matrix products, on_device(): jnp.dot(basis_rows, right_side.T, precision=highest)  34.1 us
    another operation x6, other arithmetic, orthonormal(): factor_low = jnp.linalg.cholesky(gram_total)  34 us
  transfers between devices with their start and end apart: 6, of which 6 were waited for; matrix products, arithmetic and copies ran while one was open for 0% of the time, Pallas kernels for 0%

profile of v1, /device:TPU:0, one launch (start us, length us, event | category | flops | bytes accessed | tf_op | source)
XLA Modules:
  0.0 615.5 jit_solution(6904370140503912813)
XLA Ops:
  7.2 0.0 copy-start
  7.2 0.0 all-gather.4.cloned.1.call-start
  7.2 0.7 all-gather.4.cloned.1.call-update
  7.9 0.0 all-gather.6.cloned.1.call-start
  8.0 0.7 all-gather.6.cloned.1.call-update
  8.7 0.0 all-reduce.4.cloned.1.call-start
  8.7 59.7 %all-gather.4.cloned.1.call-done = bf16[2048,1280]{1,0:T(8,128)(2,1)} async-done(((bf16[256,1280]{1,0:T(8,128)(2,1)}), bf16[2048,1280]{1,0:T(8,128)(2,1)}) %all-gather.4.cloned.1.call-update) | async-done | bytes 5242896 | tf_op jit(solution)/shard_map/all_gather | solution.py:35
  68.4 127.4 %all-gather.6.cloned.1.call-done = bf16[2048,3200]{1,0:T(8,128)(2,1)} async-done(((bf16[512,3200]{1,0:T(8,128)(2,1)}), bf16[2048,3200]{1,0:T(8,128)(2,1)}) %all-gather.6.cloned.1.call-update) | async-done | bytes 13107216 | tf_op jit(solution)/shard_map/all_gather | solution.py:38
  195.8 29.4 %convolution_add_fusion = f32[1280,3200]{1,0:T(8,128)} fusion(f32[1280,3200]{1,0:T(8,128)} %param.8, bf16[2048,1280]{1,0:T(8,128)(2,1)} %all-gather.4.cloned.1.call-done, bf16[2048,3200]{1,0:T(8,128)(2,1)} %all-gather.6.cloned.1.call-done), kind=kOutput, calls=%fused_computation.2 | convolution fusion | flops 16781312000 | bytes 51118080 | tf_op jit(solution)/shard_map/dot_general | solution.py:36
  225.1 0.0 copy-done
  225.1 17.8 %fusion.15 = f32[1280,256]{1,0:T(8,128)} fusion(f32[1280,3200]{1,0:T(8,128)} %convolution_add_fusion, f32[3200,256]{1,0:T(8,128)S(1)} %copy-done), kind=kOutput, calls=%fused_computation.41 | convolution fusion | flops 12582912000 | bytes 20971520 | tf_op jit(solution)/shard_map/dot_general | solution.py:43
  242.9 0.0 all-reduce.4.cloned.1.call-update
  242.9 0.0 all-reduce.6.cloned.1.call-start
  243.0 60.5 %all-reduce.4.cloned.1.call-done = f32[1280,256]{1,0:T(8,128)} async-done(((f32[1280,256]{1,0:T(8,128)}), f32[1280,256]{1,0:T(8,128)}) %all-reduce.4.cloned.1.call-update) | async-done | bytes 1310736 | tf_op jit(solution)/shard_map/psum | solution.py:44
  303.5 0.0 copy-start.5
  303.5 4.8 fusion.16
  308.3 0.0 all-reduce.6.cloned.1.call-update
  308.4 0.2 reduce-scatter.2.cloned.1.call-start
  308.6 42.0 %all-reduce.6.cloned.1.call-done = f32[256,256]{0,1:T(8,128)} async-done(((f32[256,256]{0,1:T(8,128)}), f32[256,256]{0,1:T(8,128)}) %all-reduce.6.cloned.1.call-update) | async-done | bytes 262160 | tf_op jit(solution)/shard_map/psum | solution.py:45
  350.6 1.1 copy.9
  351.7 1.0 fusion.5
  352.7 11.7 %cholesky.50 = f32[128,128]{1,0:T(8,128)S(1)} custom-call(f32[128,128]{1,0:T(8,128)S(1)} %cholesky.118), custom_call_target="Cholesky" | custom-call | tf_op jit(solution)/shard_map/jit(cholesky)/cholesky | solution.py:30
  364.4 9.8 %custom-call.15 = f32[1,128,128]{1,2,0:T(8,128)S(1)} custom-call(f32[1,128,128]{2,1,0:T(8,128)S(1)} %get-tuple-element.24), custom_call_target="InvertDiagBlocksLowerTriangular" | custom-call | tf_op jit(solution)/shard_map/jit(cholesky)/cholesky | solution.py:30
  374.3 0.2 constant_dynamic-update-slice_fusion.1
  374.5 0.3 convolution_subtract_fusion.1
  374.8 11.7 %cholesky.105 = f32[128,128]{1,0:T(8,128)S(1)} custom-call(f32[128,128]{1,0:T(8,128)S(1)} %convolution_subtract_fusion.1), custom_call_target="Cholesky" | custom-call | tf_op jit(solution)/shard_map/jit(cholesky)/cholesky | solution.py:30
  386.5 0.7 compare_reduce_fusion
  388.6 0.1 triangular_solve.57
  388.7 4.3 while.1
  388.9 0.6 fusion.31
  389.5 1.4 bitcast_dynamic-update-slice_fusion.2
  390.9 0.6 fusion.31
  391.5 1.4 bitcast_dynamic-update-slice_fusion.2
  392.9 19.7 %custom-call.16 = f32[2,128,128]{1,2,0:T(8,128)S(1)} custom-call(f32[2,128,128]{2,1,0:T(8,128)S(1)} %get-tuple-element.10), custom_call_target="InvertDiagBlocksLowerTriangular" | custom-call | tf_op jit(solution)/shard_map/jit(_solve_triangular)/triangular_solve | solution.py:31
  412.6 0.0 copy-done.5
  412.6 0.8 fusion.3
  413.4 0.0 copy-start.2
  413.4 1.2 convolution_subtract_fusion
  414.6 0.8 fusion.7
  415.4 0.0 copy-start.6
  415.4 32.1 %fusion.2 = f32[3200,256]{1,0:T(8,128)} fusion(f32[1280,3200]{1,0:T(8,128)} %convolution_add_fusion, f32[128,1280]{1,0:T(8,128)S(1)} %fusion.7, f32[128,1280]{1,0:T(8,128)S(1)} %fusion.3), kind=kOutput, calls=%fused_computation.11 | convolution fusion | flops 12583239680 | bytes 20971520 | tf_op jit(solution)/shard_map/dot_general | solution.py:26
  447.5 0.0 reduce-scatter.2.cloned.1.call-update
  447.5 0.0 all-gather.8.cloned.1.call-start
  447.6 45.1 %reduce-scatter.2.cloned.1.call-done = f32[800,256]{1,0:T(8,128)} async-done(((f32[3200,256]{1,0:T(8,128)}), f32[800,256]{1,0:T(8,128)}) %reduce-scatter.2.cloned.1.call-update) | async-done | bytes 819216 | tf_op jit(solution)/shard_map/reduce_scatter | solution.py:48
  492.7 0.0 all-gather.8.cloned.1.call-update
  492.7 1.3 multiply_reduce_fusion
  494.0 16.2 %psum.30 = f32[256]{0:T(256)S(1)} all-reduce(f32[256]{0:T(256)S(1)} %multiply_reduce_fusion), channel_id=1, replica_groups=mesh['row'=4,'col'=8] {'col'}, use_global_device_ids=true, to_apply=%region_8.9 | all-reduce | flops 256 | bytes 2048 | tf_op jit(solution)/shard_map/psum | solution.py:19
  510.2 8.9 %psum.31 = f32[256]{0:T(256)S(1)} all-reduce(f32[256]{0:T(256)S(1)} %psum.30), channel_id=1, replica_groups=mesh['row'=4,'col'=8] {'row'}, use_global_device_ids=true, to_apply=%region_9.10 | all-reduce | flops 256 | bytes 2048 | tf_op jit(solution)/shard_map/psum | solution.py:19
  519.1 20.3 %all-gather.8.cloned.1.call-done = f32[3200,256]{1,0:T(8,128)} async-done(((f32[800,256]{1,0:T(8,128)}), f32[3200,256]{1,0:T(8,128)}) %all-gather.8.cloned.1.call-update) | async-done | bytes 3276816 | tf_op jit(solution)/shard_map/all_gather | solution.py:50
  539.4 2.1 broadcast_multiply_fusion
  541.6 0.0 copy-done.2
  541.6 0.0 copy-done.6
  541.6 0.0 copy-start.3
  541.6 0.0 copy-start.4
  541.6 32.8 %fusion.1 = f32[1280,3200]{1,0:T(8,128)} fusion(f32[3200,256]{1,0:T(8,128)S(1)} %broadcast_multiply_fusion, bf16[1280,3200]{1,0:T(8,128)(2,1)} %param.7, f32[128,1280]{1,0:T(8,128)S(1)} %fusion.7, f32[128,1280]{1,0:T(8,128)S(1)} %fusion.3), kind=kOutput, calls=%fused_computation.6 | convolution fusion | flops 12599623680 | bytes 29163520 | tf_op jit(solution)/shard_map/dot_general | solution.py:54
  574.4 0.0 copy-done.3
  574.4 0.0 copy-done.4
  574.4 0.0 copy-start.1
  574.4 34.1 %fusion = f32[1280,3200]{1,0:T(8,128)} fusion(f32[1280,3200]{1,0:T(8,128)} %convolution_add_fusion, f32[3200,256]{1,0:T(8,128)S(1)} %copy-done.4, f32[128,1280]{1,0:T(8,128)} %copy-done.6, f32[128,1280]{1,0:T(8,128)} %copy-done.2), kind=kOutput, calls=%fused_computation.4 | convolution fusion | flops 12591431680 | bytes 37355520 | tf_op jit(solution)/shard_map/dot_general | solution.py:53
  608.5 0.0 copy-done.1
  (10 shorter events, 0.2 us)
Async XLA Ops:
  7.2 217.9 %copy-start = (f32[3200,256]{1,0:T(8,128)S(1)}, f32[3200,256]{1,0:T(8,128)}, u32[]{:S(2)}) copy-start(f32[3200,256]{1,0:T(8,128)} %param.9) | copy-start | bytes 9830404
  7.2 61.2 %all-gather.4.cloned.1.call-start = ((), (), s32[]{:S(2)}) async-start(), calls=%async_computation.1 | async-start | bytes 5898240 | tf_op jit(solution)/shard_map/all_gather | solution.py:35
  7.9 187.8 %all-gather.6.cloned.1.call-start = ((), (), s32[]{:S(2)}) async-start(), calls=%async_computation.2 | async-start | bytes 16384000 | tf_op jit(solution)/shard_map/all_gather | solution.py:38
  8.7 294.8 %all-reduce.4.cloned.1.call-start = ((), (), s32[]{:S(2)}) async-start(), calls=%async_computation.3 | async-start | bytes 2621440 | tf_op jit(solution)/shard_map/psum | solution.py:44
  242.9 107.7 %all-reduce.6.cloned.1.call-start = ((), (), s32[]{:S(2)}) async-start(), calls=%async_computation.4 | async-start | bytes 524288 | tf_op jit(solution)/shard_map/psum | solution.py:45
  303.5 109.1 %copy-start.5 = (f32[1280,256]{1,0:T(8,128)S(1)}, f32[1280,256]{1,0:T(8,128)}, u32[]{:S(2)}) copy-start(f32[1280,256]{1,0:T(8,128)} %all-reduce.4.cloned.1.call-done) | copy-start | bytes 3932164
  308.4 184.3 %reduce-scatter.2.cloned.1.call-start = ((), (), s32[]{:S(2)}) async-start(), calls=%async_computation.5 | async-start | bytes 4096000 | tf_op jit(solution)/shard_map/reduce_scatter | solution.py:48
  413.4 128.2 %copy-start.2 = (f32[128,1280]{1,0:T(8,128)}, f32[128,1280]{1,0:T(8,128)S(1)}, u32[]{:S(2)}) copy-start(f32[128,1280]{1,0:T(8,128)S(1)} %fusion.3) | copy-start | bytes 1966084
  415.4 126.2 %copy-start.6 = (f32[128,1280]{1,0:T(8,128)}, f32[128,1280]{1,0:T(8,128)S(1)}, u32[]{:S(2)}) copy-start(f32[128,1280]{1,0:T(8,128)S(1)} %fusion.7) | copy-start | bytes 1966084
  447.5 91.9 %all-gather.8.cloned.1.call-start = ((), (), s32[]{:S(2)}) async-start(), calls=%async_computation.6 | async-start | bytes 4096000 | tf_op jit(solution)/shard_map/all_gather | solution.py:50
  541.6 32.8 %copy-start.3 = (f32[3200,256]{1,0:T(8,128)}, f32[3200,256]{1,0:T(8,128)S(1)}, u32[]{:S(2)}) copy-start(f32[3200,256]{1,0:T(8,128)S(1)} %broadcast_multiply_fusion) | copy-start | bytes 9830404
  541.6 32.8 %copy-start.4 = (f32[3200,256]{1,0:T(8,128)S(1)}, f32[3200,256]{1,0:T(8,128)}, u32[]{:S(2)}) copy-start(f32[3200,256]{1,0:T(8,128)} %all-gather.8.cloned.1.call-done) | copy-start | bytes 9830404
  574.4 34.1 %copy-start.1 = (f32[3200,256]{1,0:T(8,128)S(1)}, f32[3200,256]{1,0:T(8,128)}, u32[]{:S(2)}) copy-start(f32[3200,256]{1,0:T(8,128)} %param.9) | copy-start | bytes 9830404
Sparse Core Ops, SparseCore 0:
  9.6 58.6 all-gather.3
  70.2 125.5 all-gather.5
  243.0 60.4 all-reduce.3
  308.5 42.0 all-reduce.5
  447.6 44.9 reduce-scatter.1
  494.4 45.0 all-gather.7
